TPU v7x, 32 devices: a whole 2x2x4 slice. The times are simulated.
32 devices in a mesh: group: 2 (over x), expert: 8 (over z, y), cuts: 2 (over core).
Axes of the slice: x: 2, y: 2, z: 4, core: 2. Of those that a mesh axis runs over, the one named last changes fastest.
Arguments:
- x_in: bfloat16 [512, 4096], P(('group', 'expert'), 'cuts'), parts along dimension 0, may hold values from -6 to 6
- routes: int32 [512, 2], P(('group', 'expert')), parts along dimension 0, may hold values from 0 to 15, as said below
- conv_state: float32 [64, 3, 4096], P('group', None, ('expert', 'cuts')), parts along dimension 0, may hold values from -6 to 6
- ssm_state: float32 [64, 16, 4096], P('group', None, ('expert', 'cuts')), parts along dimension 0, may hold values from -6 to 6
- mamba_gain: float32 [4096], replicated, may hold values from 0.1 to 1.9
- in_x: bfloat16 [4096, 4096], P(None, ('expert', 'cuts')), may hold values from -0.09375 to 0.09375
- in_z: bfloat16 [4096, 4096], P(None, ('expert', 'cuts')), may hold values from -0.09375 to 0.09375
- conv_w: float32 [4, 4096], P(None, ('expert', 'cuts')), may hold values from -3 to 3
- conv_b: float32 [4096], P(('expert', 'cuts')), may hold values from -3 to 3
- xproj_dt: bfloat16 [4096, 512], P(('expert', 'cuts')), may hold values from -0.09375 to 0.09375
- xproj_bc: bfloat16 [4096, 32], P(('expert', 'cuts')), may hold values from -0.09375 to 0.09375
- dt_proj: bfloat16 [512, 4096], P(None, ('expert', 'cuts')), may hold values from -0.25 to 0.25
- dt_bias: float32 [4096], P(('expert', 'cuts')), may hold values from -4 to 0
- a_rate: float32 [16, 4096], P(None, ('expert', 'cuts')), may hold values from 0.5 to 16
- d_skip: float32 [4096], P(('expert', 'cuts')), may hold values from 0.5 to 1.5
- out_proj: bfloat16 [4096, 4096], P(('expert', 'cuts')), may hold values from -0.09375 to 0.09375
- moe_gain: float32 [4096], replicated, may hold values from 0.1 to 1.9
- router: bfloat16 [4096, 16], replicated, may hold values from -0.09375 to 0.09375
- w_gate: bfloat16 [4096, 12288], P(None, ('expert', 'cuts')), may hold values from -0.09375 to 0.09375
- w_up: bfloat16 [4096, 12288], P(None, ('expert', 'cuts')), may hold values from -0.09375 to 0.09375
- w_down: bfloat16 [12288, 4096], P(('expert', 'cuts')), may hold values from -0.078125 to 0.078125
Outputs:
- stream_out: bfloat16 [512, 4096], P(('group', 'expert'), 'cuts'), parts along dimension 0
- new_state: float32 [64, 16, 4096], P('group', None, ('expert', 'cuts')), parts along dimension 0
There are 2 independent parts, one for each index of `group`. A program takes and returns all parts, laid end to end along the dimension named above; an argument that names none is the same for every part. Nothing has to cross between parts.
Inputs may be any that keep to these rules, and one draw needn't show every extreme that they name: `routes`: each token names 2 different experts. Among the 32 tokens of one index of expert (aligned blocks of rows), at most 16 name any one expert below 2, and in every block one of them is named by exactly 16; no token names two experts below 2.
All inputs are finite; a program needn't handle non-finite values.
Results may differ from a plain program's by a relative error of at most 0.0095.
Values may be sent and summed in bfloat16 or wider, within the bound.
No kernel may reach another device: no remote copies, remote signals or barrier semaphores. Data moves between devices by JAX's collectives and lax.ppermute only.
A program may use at most 128 MiB of HBM per device.

v0:
```python
import jax
import jax.numpy as jnp
from jax import lax
from jax.sharding import PartitionSpec as P

EXPERTS = 2
DRAFT = 8
CAP = 16


def rms_norm(values, gain):
    values = values.astype(jnp.float32)
    scale = lax.rsqrt(jnp.mean(values * values, axis=-1, keepdims=True) + 1e-05)
    return (values * scale * gain).astype(jnp.bfloat16)


def ssm_steps(inputs, steps, b_maps, c_maps, state, a_rate, d_skip):
    outputs = []
    for place in range(inputs.shape[1]):
        decay = jnp.exp(-steps[:, place, None, :] * a_rate[None])
        state = (
            decay * state
            + (steps[:, place] * inputs[:, place])[:, None, :] * b_maps[:, place, :, None]
        )
        outputs.append(
            jnp.sum(c_maps[:, place, :, None] * state, axis=1) + d_skip * inputs[:, place]
        )
    return (jnp.stack(outputs, axis=1), state)


def on_device(
    x_in,
    routes,
    conv_state,
    ssm_state,
    mamba_gain,
    in_x,
    in_z,
    conv_w,
    conv_b,
    xproj_dt,
    xproj_bc,
    dt_proj,
    dt_bias,
    a_rate,
    d_skip,
    out_proj,
    moe_gain,
    router,
    w_gate,
    w_up,
    w_down,
):
    tok_count, half_width = x_in.shape
    requests = conv_state.shape[0]
    channels = in_x.shape[1]
    states = a_rate.shape[0]
    topk = routes.shape[1]
    owners = lax.axis_size("expert")
    pieces = lax.axis_size("cuts")
    full_x = lax.all_gather(x_in, "cuts", axis=1, tiled=True)
    normed = rms_norm(lax.all_gather(full_x, "expert", axis=0, tiled=True), mamba_gain)
    upper = jnp.dot(normed, in_x, preferred_element_type=jnp.float32)
    lower = jnp.dot(normed, in_z, preferred_element_type=jnp.float32)
    both = jnp.stack([upper, lower])
    u_pre = both[0]
    z_gate = both[1]
    seq = jnp.concatenate([conv_state, u_pre.reshape(requests, DRAFT, channels)], axis=1)
    conv = jnp.zeros((requests, DRAFT, channels), jnp.float32) + conv_b
    for tap in range(conv_w.shape[0]):
        conv = conv + conv_w[tap] * seq[:, tap : tap + DRAFT]
    u_act = jax.nn.silu(conv).astype(jnp.bfloat16)
    flat_u = u_act.reshape(requests * DRAFT, channels)
    dt_part = jnp.dot(flat_u, xproj_dt, preferred_element_type=jnp.float32)
    map_part = jnp.dot(flat_u, xproj_bc, preferred_element_type=jnp.float32)
    dt_low, maps = lax.psum((dt_part, map_part), ("expert", "cuts"))
    steps = jax.nn.softplus(
        jnp.dot(dt_low.astype(jnp.bfloat16), dt_proj, preferred_element_type=jnp.float32) + dt_bias
    )
    b_maps = maps[:, :states].reshape(requests, DRAFT, states)
    c_maps = maps[:, states:].reshape(requests, DRAFT, states)
    outputs, new_state = ssm_steps(
        u_act.astype(jnp.float32),
        steps.reshape(requests, DRAFT, channels),
        b_maps,
        c_maps,
        ssm_state,
        a_rate,
        d_skip,
    )
    gated = (outputs.reshape(requests * DRAFT, channels) * jax.nn.silu(z_gate)).astype(jnp.bfloat16)
    term = jnp.einsum(
        "etc,ckf->ektf",
        gated.reshape(owners, tok_count, channels),
        out_proj.reshape(channels, pieces, half_width),
        preferred_element_type=jnp.float32,
    )
    term = term.reshape(owners * pieces * tok_count, half_width)
    mixed_half = lax.psum_scatter(term, ("expert", "cuts"), scatter_dimension=0, tiled=True)
    stream_half = (x_in.astype(jnp.float32) + mixed_half).astype(jnp.bfloat16)
    stream = lax.all_gather(stream_half, "cuts", axis=1, tiled=True)
    normed2 = rms_norm(stream, moe_gain)
    logits = jnp.dot(normed2, router, preferred_element_type=jnp.float32)
    all_labels = jnp.arange(router.shape[1], dtype=jnp.int32)
    pick = (routes[:, :, None] == all_labels).astype(jnp.float32)
    chosen = jnp.sum(logits[:, None, :] * pick, axis=-1)
    weight0 = jax.nn.sigmoid(chosen[:, 0] - chosen[:, 1])
    labels = jnp.arange(EXPERTS, dtype=jnp.int32)
    flat_routes = routes.reshape(tok_count * topk)
    onehot = (flat_routes[:, None] == labels).astype(jnp.int32)
    rank = jnp.cumsum(onehot, axis=0) - 1
    slot = jnp.sum(rank * onehot, axis=-1)
    inside = jnp.sum(onehot, axis=-1)
    dest = jnp.where(inside > 0, flat_routes * CAP + slot, EXPERTS * CAP)
    row_width = normed2.shape[1]
    rows = jnp.repeat(normed2, topk, axis=0)
    buffer = (
        jnp.zeros((EXPERTS * CAP + 1, row_width), jnp.bfloat16).at[dest].set(rows)[: EXPERTS * CAP]
    )
    buffer = buffer.reshape(EXPERTS, CAP, row_width)
    holders = owners // EXPERTS
    outgoing = jnp.repeat(buffer, holders, axis=0)[:, None]
    received = lax.all_to_all(outgoing, "expert", split_axis=0, concat_axis=1, tiled=True)
    local, sources, count, features = received.shape
    tokens = received.reshape(local * sources * count, features)
    gate = jnp.dot(tokens, w_gate, preferred_element_type=jnp.float32)
    upval = jnp.dot(tokens, w_up, preferred_element_type=jnp.float32)
    act = (jax.nn.silu(gate) * upval).astype(jnp.bfloat16)
    partial_out = jnp.dot(act, w_down, preferred_element_type=jnp.float32)
    partial_out = partial_out.reshape(local, sources, count, features)
    returned = lax.all_to_all(
        partial_out.astype(jnp.bfloat16), "expert", split_axis=1, concat_axis=0, tiled=True
    ).astype(partial_out.dtype)
    back_width = returned.shape[3]
    grouped = jnp.sum(returned.reshape(EXPERTS, holders, CAP, back_width), axis=1).reshape(
        EXPERTS * CAP, back_width
    )
    table = jnp.concatenate([grouped, jnp.zeros((1, back_width), jnp.float32)], axis=0)
    picked = table[dest].reshape(tok_count, topk, back_width)
    expert_out = lax.psum_scatter(
        picked.astype(jnp.bfloat16), "cuts", scatter_dimension=2, tiled=True
    )
    expert_out = expert_out.astype(jnp.float32)
    total = (
        stream_half.astype(jnp.float32)
        + weight0[:, None] * expert_out[:, 0]
        + (1.0 - weight0)[:, None] * expert_out[:, 1]
    )
    return (total.astype(jnp.bfloat16), new_state)


def solution(mesh):
    return jax.shard_map(
        on_device,
        mesh=mesh,
        in_specs=(
            P(("group", "expert"), "cuts"),
            P(("group", "expert"), None),
            P("group", None, ("expert", "cuts")),
            P("group", None, ("expert", "cuts")),
            P(),
            P(None, ("expert", "cuts")),
            P(None, ("expert", "cuts")),
            P(None, ("expert", "cuts")),
            P(("expert", "cuts")),
            P(("expert", "cuts"), None),
            P(("expert", "cuts"), None),
            P(None, ("expert", "cuts")),
            P(("expert", "cuts")),
            P(None, ("expert", "cuts")),
            P(("expert", "cuts")),
            P(("expert", "cuts"), None),
            P(),
            P(),
            P(None, ("expert", "cuts")),
            P(None, ("expert", "cuts")),
            P(("expert", "cuts"), None),
        ),
        out_specs=(P(("group", "expert"), "cuts"), P("group", None, ("expert", "cuts"))),
        check_vma=False,
    )
```

profile of v0, /device:TPU:0, one launch (start us, length us, event | category | flops | bytes accessed | tf_op | source)
XLA Modules:
  0.0 318.8 jit_solution(7484145724764435932)
XLA Ops:
  7.2 4.1 %all_gather.9 = bf16[32,4096]{1,0:T(8,128)(2,1)} all-gather(bf16[32,2048]{1,0:T(8,128)(2,1)} %param.21), channel_id=1, replica_groups=mesh['group'=2,'expert'=8,'cuts'=2] {'cuts'}, dimensions={1}, use_global_device_ids=true | all-gather | bytes 393216 | tf_op jit(solution)/shard_map/all_gather | solution.py:61
  11.4 1.0 copy.129
  12.3 0.8 fusion.51
  13.2 50.0 %all-gather.2.cloned.1.call-done = bf16[256,4096]{1,0:T(8,128)(2,1)} async-done(((bf16[32,4096]{1,0:T(8,128)(2,1)}), bf16[256,4096]{1,0:T(8,128)(2,1)}) %all-gather.2.cloned.1.call-update) | async-done | bytes 2097168 | tf_op jit(solution)/shard_map/all_gather | solution.py:62
  63.2 2.1 fusion
  65.4 2.4 convolution_bitcast_fusion
  68.4 65.3 %all-reduce.3 = (f32[256,32]{0,1:T(8,128)S(1)}, bf16[256,512]{1,0:T(8,128)(2,1)}) all-reduce(f32[256,32]{0,1:T(8,128)S(1)} %fusion.41, f32[256,512]{1,0:T(8,128)S(1)} %fusion.39), channel_id=1, replica_groups=mesh['group'=2,'expert'=8,'cuts'=2] {'expert','cuts'}, use_global_device_ids=true, to_apply=%region_1.2 | all-reduce | flops 139264 | bytes 851968 | tf_op jit(solution)/shard_map/psum | solution.py:76
  133.8 1.3 fusion.25
  135.9 1.1 slice_multiply_fusion.4
  138.0 0.8 copy_bitcast_fusion.10
  139.6 0.8 copy_bitcast_fusion.11
  140.3 0.8 copy_bitcast_fusion.5
  141.8 2.5 multiply_reduce_fusion
  144.3 0.9 multiply_reduce_fusion.1
  145.2 1.0 multiply_add_fusion.8
  146.6 3.2 fusion.32
  149.8 2.6 fusion.3
  153.3 69.0 %reduce-scatter.3.cloned.1.call-done = f32[32,2048]{1,0:T(8,128)} async-done(((f32[512,2048]{1,0:T(8,128)}), f32[32,2048]{1,0:T(8,128)}) %reduce-scatter.3.cloned.1.call-update) | async-done | bytes 262160 | tf_op jit(solution)/shard_map/reduce_scatter | solution.py:99
  222.3 1.0 add_convert_fusion
  223.3 2.0 all_gather.11
  226.3 1.4 scatter_custom_fusion
  227.8 29.6 %all_to_all.8 = bf16[8,1,16,4096]{3,2,1,0:T(8,128)(2,1)S(1)} all-to-all(bf16[8,1,16,4096]{3,2,1,0:T(8,128)(2,1)S(1)} %bitcast.143), channel_id=1, replica_groups=mesh['group'=2,'expert'=8,'cuts'=2] {'expert'}, dimensions={0} | all-to-all | bytes 2097152 | tf_op jit(solution)/shard_map/all_to_all | solution.py:123
  257.3 4.5 %fusion.53 = f32[128,768]{1,0:T(8,128)} fusion(bf16[128,4096]{1,0:T(8,128)(2,1)S(1)} %bitcast.139, bf16[4096,768]{1,0:T(8,128)(2,1)} %param.39), kind=kOutput, calls=%fused_computation.141 | convolution fusion | flops 805306368 | bytes 7733248 | tf_op jit(solution)/shard_map/dot_general | solution.py:126
  261.9 8.2 %convolution_convert_fusion = bf16[128,4096]{1,0:T(8,128)(2,1)} fusion(bf16[768,4096]{1,0:T(8,128)(2,1)} %param.41, bf16[128,4096]{1,0:T(8,128)(2,1)S(1)} %bitcast.140, bf16[4096,768]{1,0:T(8,128)(2,1)} %param.40, f32[128,768]{1,0:T(8,128)} %fusion.53), kind=kOutput, calls=%fused_computation.4 | convolution fusion | flops 1611726848 | bytes 15073280 | tf_op jit(solution)/shard_map/dot_general | solution.py:129
  270.0 3.6 %all-to-all-start.1 = ((bf16[1,8,16,4096]{3,2,0,1:T(8,128)(2,1)}), bf16[1,8,16,4096]{3,2,0,1:T(8,128)(2,1)S(1)}, u32[]{:S(2)}, u32[]{:S(2)}) async-start(bf16[1,8,16,4096]{3,2,0,1:T(8,128)(2,1)} %bitcast.141), calls=%async_computation.2 | async-start | bytes 2097152 | tf_op jit(solution)/shard_map/all_to_all | solution.py:131
  273.7 25.5 %all-to-all-done.1 = bf16[1,8,16,4096]{3,2,0,1:T(8,128)(2,1)S(1)} async-done(((bf16[1,8,16,4096]{3,2,0,1:T(8,128)(2,1)}), bf16[1,8,16,4096]{3,2,0,1:T(8,128)(2,1)S(1)}, u32[]{:S(2)}, u32[]{:S(2)}) %all-to-all-start.1) | async-done | bytes 1048608 | tf_op jit(solution)/shard_map/all_to_all | solution.py:131
  299.5 0.9 gather_fusion
  300.3 1.2 convert_element_type.97
  301.5 2.1 copy.168
  303.9 6.7 %reduce-scatter.5.cloned.1.call-done = bf16[32,2,2048]{2,0,1:T(8,128)(2,1)} async-done(((bf16[32,2,4096]{2,0,1:T(8,128)(2,1)}), bf16[32,2,2048]{2,0,1:T(8,128)(2,1)}) %reduce-scatter.5.cloned.1.call-update) | async-done | bytes 262160 | tf_op jit(solution)/shard_map/reduce_scatter | solution.py:140
  310.5 1.0 convert_element_type.98
  311.5 0.8 fusion.28
  (71 shorter events, 6.7 us)
Async XLA Ops:
  7.2 58.2 %copy-start = (bf16[4096,256]{1,0:T(8,128)(2,1)S(1)}, bf16[4096,256]{1,0:T(8,128)(2,1)}, u32[]{:S(2)}) copy-start(bf16[4096,256]{1,0:T(8,128)(2,1)} %param.26) | copy-start | bytes 6291460
  7.2 56.0 %all-gather.2.cloned.1.call-start = ((), (), s32[]{:S(2)}) async-start(), calls=%async_computation.4 | async-start | bytes 2359296 | tf_op jit(solution)/shard_map/all_gather | solution.py:62
  11.3 211.0 %reduce-scatter.3.cloned.1.call-start = ((), (), s32[]{:S(2)}) async-start(), calls=%async_computation.5 | async-start | bytes 4456448 | tf_op jit(solution)/shard_map/reduce_scatter | solution.py:99
  13.2 54.6 %copy-start.10 = (f32[256]{0:T(256)S(1)}, f32[256]{0:T(256)}, u32[]{:S(2)}) copy-start(f32[256]{0:T(256)} %param.29) | copy-start | bytes 3076
  63.2 4.8 %copy-start.4 = (bf16[256,512]{1,0:T(8,128)(2,1)S(1)}, bf16[256,512]{1,0:T(8,128)(2,1)}, u32[]{:S(2)}) copy-start(bf16[256,512]{1,0:T(8,128)(2,1)} %param.30) | copy-start | bytes 786436
  65.3 3.0 copy-start.8
  65.4 2.9 copy-start.11
  65.4 68.4 %copy-start.12 = (f32[256]{0:T(256)S(1)}, f32[256]{0:T(256)}, u32[]{:S(2)}) copy-start(f32[256]{0:T(256)} %param.33) | copy-start | bytes 3076
  67.7 73.4 %copy-start.2 = (f32[32,16,256]{2,1,0:T(8,128)S(1)}, f32[32,16,256]{2,1,0:T(8,128)}, u32[]{:S(2)}) copy-start(f32[32,16,256]{2,1,0:T(8,128)} %param.24) | copy-start | bytes 1572868
  67.8 73.4 %copy-start.5 = (f32[16,256]{1,0:T(8,128)S(1)}, f32[16,256]{1,0:T(8,128)}, u32[]{:S(2)}) copy-start(f32[16,256]{1,0:T(8,128)} %param.34) | copy-start | bytes 49156
  146.6 3.2 %copy-start.1 = (bf16[256,4096]{1,0:T(8,128)(2,1)S(1)}, bf16[256,4096]{1,0:T(8,128)(2,1)}, u32[]{:S(2)}) copy-start(bf16[256,4096]{1,0:T(8,128)(2,1)} %param.36) | copy-start | bytes 6291460
  149.8 2.7 copy-start.9
  149.8 72.5 %copy-start.3 = (bf16[32,2048]{1,0:T(8,128)(2,1)S(1)}, bf16[32,2048]{1,0:T(8,128)(2,1)}, u32[]{:S(2)}) copy-start(bf16[32,2048]{1,0:T(8,128)(2,1)} %param.21) | copy-start | bytes 393220
  152.5 73.0 %copy-start.7 = (f32[4096]{0:T(1024)S(1)}, f32[4096]{0:T(1024)}, u32[]{:S(2)}) copy-start(f32[4096]{0:T(1024)} %param.37) | copy-start | bytes 49156
  270.0 29.2 %all-to-all-start.1 = ((bf16[1,8,16,4096]{3,2,0,1:T(8,128)(2,1)}), bf16[1,8,16,4096]{3,2,0,1:T(8,128)(2,1)S(1)}, u32[]{:S(2)}, u32[]{:S(2)}) async-start(bf16[1,8,16,4096]{3,2,0,1:T(8,128)(2,1)} %bitcast.141), calls=%async_computation.2 | async-start | bytes 2097152 | tf_op jit(solution)/shard_map/all_to_all | solution.py:131
  273.7 36.9 %reduce-scatter.5.cloned.1.call-start = ((), (), s32[]{:S(2)}) async-start(), calls=%async_computation.6 | async-start | bytes 786432 | tf_op jit(solution)/shard_map/reduce_scatter | solution.py:140
  299.4 4.2 %copy-start.6 = (bf16[4096,16]{0,1:T(8,128)(2,1)S(1)}, bf16[4096,16]{0,1:T(8,128)(2,1)}, u32[]{:S(2)}) copy-start(bf16[4096,16]{0,1:T(8,128)(2,1)} %param.38) | copy-start | bytes 393220
Sparse Core Ops, SparseCore 0:
  11.5 51.7 all-gather.1
  152.6 69.6 reduce-scatter.2
  303.7 6.7 reduce-scatter.4
where the time goes:
time: 320 us; the launch traced here: 319 us
  waiting for transfers between devices  151 us (47%)
  blocking collectives  101 us (32%)
  matrix products  22.8 us (7%)
  between operations  14.1 us (4%)
  local copies, waits for them, and re-layouts  13.1 us (4%)
  other arithmetic  12.9 us (4%)
  starting transfers between devices  3.76 us (1%)
    reduce_scatter x1, waiting for transfers between devices, on_device(): lax.psum_scatter(term, ('expert', 'cuts'), scatter_dimension=0, tiled=True)  69 us
    psum x1, blocking collectives, on_device(): dt_low, maps = lax.psum((dt_part, map_part), ('expert', 'cuts'))  65.3 us
    all_gather x1, waiting for transfers between devices, on_device(): lax.all_gather(full_x, 'expert', axis=0, tiled=True)  50 us
    all_to_all x1, blocking collectives, on_device(): lax.all_to_all(outgoing, 'expert', split_axis=0, concat_axis=1, tiled=True)  29.6 us
    all_to_all x1, waiting for transfers between devices, on_device(): lax.all_to_all(partial_out.astype(jnp.bfloat16), 'expert', split_axis=1,...  25.5 us
    dot_general x1, matrix products, on_device(): partial_out = jnp.dot(act, w_down, preferred_element_type=jnp.float32)  8.17 us
    reduce_scatter x1, waiting for transfers between devices, on_device(): lax.psum_scatter(picked.astype(jnp.bfloat16), 'cuts', scatter_dimension=2...  6.68 us
  transfers between devices with their start and end apart: 4, of which 4 were waited for; matrix products, arithmetic and copies ran while one was open for 1% of the time, Pallas kernels for 0%

commit v1 on v0

--- a/solution.py
+++ b/solution.py
@@ -6,6 +6,27 @@
 EXPERTS = 2
 DRAFT = 8
 CAP = 16
+
+
+def collect(value, axis, dim):
+    count, here, width = (lax.axis_size(axis), lax.axis_index(axis), value.shape[dim])
+    ahead = [(i, (i + 1) % count) for i in range(count)]
+    downward = [(i, (i - 1) % count) for i in range(count)]
+    whole = jnp.zeros((*value.shape[:dim], count * width, *value.shape[dim + 1 :]), value.dtype)
+    whole = lax.dynamic_update_slice_in_dim(whole, value, here * width, axis=dim)
+    from_left = from_right = value
+    half = count // 2
+    for step in range(1, half + 1):
+        from_left = lax.ppermute(from_left, axis, ahead)
+        whole = lax.dynamic_update_slice_in_dim(
+            whole, from_left, (here - step) % count * width, axis=dim
+        )
+        if step < count - half:
+            from_right = lax.ppermute(from_right, axis, downward)
+            whole = lax.dynamic_update_slice_in_dim(
+                whole, from_right, (here + step) % count * width, axis=dim
+            )
+    return whole
 
 
 def rms_norm(values, gain):
@@ -59,7 +80,7 @@
     owners = lax.axis_size("expert")
     pieces = lax.axis_size("cuts")
     full_x = lax.all_gather(x_in, "cuts", axis=1, tiled=True)
-    normed = rms_norm(lax.all_gather(full_x, "expert", axis=0, tiled=True), mamba_gain)
+    normed = rms_norm(collect(full_x, "expert", 0), mamba_gain)
     upper = jnp.dot(normed, in_x, preferred_element_type=jnp.float32)
     lower = jnp.dot(normed, in_z, preferred_element_type=jnp.float32)
     both = jnp.stack([upper, lower])

time: 320 us -> 313 us (0.978)
  waiting for transfers between devices: 151 us -> 124 us
  starting transfers between devices: 3.76 us -> 23.1 us
  local copies, waits for them, and re-layouts: 13.1 us -> 19.1 us
    all_gather x1 -> x0, waiting for transfers between devices: 50 us -> none  [on_device(): lax.all_gather(full_x, 'expert', axis=0, tiled=True)]
    ppermute x0 -> x7, waiting for transfers between devices: none -> 23.5 us  [the longest x4 23.5 us: collect(): from_left = lax.ppermute(from_left, axis, ahead)]
    ppermute x0 -> x7, starting transfers between devices: none -> 19.4 us  [the longest x4 10.3 us: collect(): from_left = lax.ppermute(from_left, axis, ahead)]
    dynamic_update_slice x0 -> x8, local copies, waits for them, and re-layouts: none -> 5.73 us  [the longest x4 2.9 us: collect(): lax.dynamic_update_slice_in_dim(whole, from_left, (here - step) % count *...]
  transfers between devices with their start and end apart: 4 -> 10, of which waited for: 4 -> 7; matrix products, arithmetic and copies ran while one was open for 1% -> 2% of each run, Pallas kernels for 0% -> 0%
where the time goes in v1:
time: 313 us
  waiting for transfers between devices  124 us (40%)
  blocking collectives  98.3 us (31%)
  starting transfers between devices  23.1 us (7%)
  matrix products  22.8 us (7%)
  local copies, waits for them, and re-layouts  19.1 us (6%)
  between operations  14.6 us (5%)
  other arithmetic  10.8 us (3%)
    reduce_scatter x1, waiting for transfers between devices, on_device(): lax.psum_scatter(term, ('expert', 'cuts'), scatter_dimension=0, tiled=True)  68.4 us
    psum x1, blocking collectives, on_device(): dt_low, maps = lax.psum((dt_part, map_part), ('expert', 'cuts'))  64.3 us
    all_to_all x1, blocking collectives, on_device(): lax.all_to_all(outgoing, 'expert', split_axis=0, concat_axis=1, tiled=True)  29.5 us
    all_to_all x1, waiting for transfers between devices, on_device(): lax.all_to_all(partial_out.astype(jnp.bfloat16), 'expert', split_axis=1,...  25.5 us
    ppermute x4, waiting for transfers between devices, collect(): from_left = lax.ppermute(from_left, axis, ahead)  23.5 us
    ppermute x4, starting transfers between devices, collect(): from_left = lax.ppermute(from_left, axis, ahead)  10.3 us
    ppermute x3, starting transfers between devices, collect(): from_right = lax.ppermute(from_right, axis, downward)  9.12 us
    dot_general x1, matrix products, on_device(): partial_out = jnp.dot(act, w_down, preferred_element_type=jnp.float32)  8.15 us
  transfers between devices with their start and end apart: 10, of which 7 were waited for; matrix products, arithmetic and copies ran while one was open for 2% of the time, Pallas kernels for 0%

profile of v1, /device:TPU:0, one launch (start us, length us, event | category | flops | bytes accessed | tf_op | source)
XLA Modules:
  0.0 312.8 jit_solution(7064053719413192031)
XLA Ops:
  7.2 2.5 all_gather.6
  9.8 2.9 collective-permute-start
  12.6 3.0 collective-permute-start.1
  15.7 1.6 broadcast_in_dim.11
  18.1 6.1 %collective-permute-done = bf16[32,4096]{1,0:T(8,128)(2,1)S(1)} collective-permute-done((bf16[32,4096]{1,0:T(8,128)(2,1)S(1)}, bf16[32,4096]{1,0:T(8,128)(2,1)S(1)}, u32[]{:S(2)}, u32[]{:S(2)}) %collective-permute-start) | collective-permute-done | bytes 262176 | tf_op jit(solution)/shard_map/ppermute | solution.py:20
  24.2 2.5 collective-permute-start.2
  26.6 3.0 collective-permute-start.3
  31.1 6.2 %collective-permute-done.2 = bf16[32,4096]{1,0:T(8,128)(2,1)S(1)} collective-permute-done((bf16[32,4096]{1,0:T(8,128)(2,1)S(1)}, bf16[32,4096]{1,0:T(8,128)(2,1)S(1)}, u32[]{:S(2)}, u32[]{:S(2)}) %collective-permute-start.2) | collective-permute-done | bytes 262176 | tf_op jit(solution)/shard_map/ppermute | solution.py:20
  37.3 2.5 collective-permute-start.4
  39.8 3.0 collective-permute-start.5
  44.3 5.5 %collective-permute-done.4 = bf16[32,4096]{1,0:T(8,128)(2,1)S(1)} collective-permute-done((bf16[32,4096]{1,0:T(8,128)(2,1)S(1)}, bf16[32,4096]{1,0:T(8,128)(2,1)S(1)}, u32[]{:S(2)}, u32[]{:S(2)}) %collective-permute-start.4) | collective-permute-done | bytes 262176 | tf_op jit(solution)/shard_map/ppermute | solution.py:20
  49.7 2.5 collective-permute-start.6
  53.7 5.8 %collective-permute-done.6 = bf16[32,4096]{1,0:T(8,128)(2,1)S(1)} collective-permute-done((bf16[32,4096]{1,0:T(8,128)(2,1)S(1)}, bf16[32,4096]{1,0:T(8,128)(2,1)S(1)}, u32[]{:S(2)}, u32[]{:S(2)}) %collective-permute-start.6) | collective-permute-done | bytes 262176 | tf_op jit(solution)/shard_map/ppermute | solution.py:20
  60.2 2.1 fusion
  62.3 2.4 convolution_bitcast_fusion
  65.4 64.3 %all-reduce.3 = (f32[256,32]{0,1:T(8,128)S(1)}, bf16[256,512]{1,0:T(8,128)(2,1)}) all-reduce(f32[256,32]{0,1:T(8,128)S(1)} %fusion.41, f32[256,512]{1,0:T(8,128)S(1)} %fusion.39), channel_id=1, replica_groups=mesh['group'=2,'expert'=8,'cuts'=2] {'expert','cuts'}, use_global_device_ids=true, to_apply=%region_1.2 | all-reduce | flops 139264 | bytes 851968 | tf_op jit(solution)/shard_map/psum | solution.py:97
  129.7 1.3 fusion.25
  136.9 1.8 multiply_reduce_fusion
  140.4 3.2 %fusion.32 = bf16[256,256]{1,0:T(8,128)(2,1)S(1)} fusion(f32[32,8,256]{2,1,0:T(8,128)S(1)} %stack.2, bf16[4096,256]{1,0:T(8,128)(2,1)} %param.27, bf16[256,4096]{1,0:T(8,128)(2,1)} %constant_dynamic-update-slice_fusion, f32[4096]{0:T(1024)S(1)} %copy-done.20, f32[256]{0:T(256)S(1)} %copy-done.17), kind=kOutput, calls=%fused_computation.67 | convolution fusion | flops 541458432 | bytes 4604928 | tf_op jit(solution)/shard_map/dot_general | solution.py:85
  143.5 2.7 fusion.3
  147.6 68.4 %reduce-scatter.3.cloned.1.call-done = f32[32,2048]{1,0:T(8,128)} async-done(((f32[512,2048]{1,0:T(8,128)}), f32[32,2048]{1,0:T(8,128)}) %reduce-scatter.3.cloned.1.call-update) | async-done | bytes 262160 | tf_op jit(solution)/shard_map/reduce_scatter | solution.py:120
  217.0 2.0 all_gather.7
  220.0 1.4 scatter_custom_fusion
  221.5 29.5 %all_to_all.8 = bf16[8,1,16,4096]{3,2,1,0:T(8,128)(2,1)S(1)} all-to-all(bf16[8,1,16,4096]{3,2,1,0:T(8,128)(2,1)S(1)} %bitcast.143), channel_id=1, replica_groups=mesh['group'=2,'expert'=8,'cuts'=2] {'expert'}, dimensions={0} | all-to-all | bytes 2097152 | tf_op jit(solution)/shard_map/all_to_all | solution.py:144
  251.0 4.5 %fusion.53 = f32[128,768]{1,0:T(8,128)} fusion(bf16[128,4096]{1,0:T(8,128)(2,1)S(1)} %bitcast.139, bf16[4096,768]{1,0:T(8,128)(2,1)} %param.39), kind=kOutput, calls=%fused_computation.149 | convolution fusion | flops 805306368 | bytes 7733248 | tf_op jit(solution)/shard_map/dot_general | solution.py:147
  255.6 8.2 %convolution_convert_fusion = bf16[128,4096]{1,0:T(8,128)(2,1)} fusion(bf16[768,4096]{1,0:T(8,128)(2,1)} %param.41, bf16[128,4096]{1,0:T(8,128)(2,1)S(1)} %bitcast.140, bf16[4096,768]{1,0:T(8,128)(2,1)} %param.40, f32[128,768]{1,0:T(8,128)} %fusion.53), kind=kOutput, calls=%fused_computation.4 | convolution fusion | flops 1611726848 | bytes 15073280 | tf_op jit(solution)/shard_map/dot_general | solution.py:150
  263.7 3.6 %all-to-all-start.1 = ((bf16[1,8,16,4096]{3,2,0,1:T(8,128)(2,1)}), bf16[1,8,16,4096]{3,2,0,1:T(8,128)(2,1)S(1)}, u32[]{:S(2)}, u32[]{:S(2)}) async-start(bf16[1,8,16,4096]{3,2,0,1:T(8,128)(2,1)} %bitcast.141), calls=%async_computation.2 | async-start | bytes 2097152 | tf_op jit(solution)/shard_map/all_to_all | solution.py:152
  267.4 25.5 %all-to-all-done.1 = bf16[1,8,16,4096]{3,2,0,1:T(8,128)(2,1)S(1)} async-done(((bf16[1,8,16,4096]{3,2,0,1:T(8,128)(2,1)}), bf16[1,8,16,4096]{3,2,0,1:T(8,128)(2,1)S(1)}, u32[]{:S(2)}, u32[]{:S(2)}) %all-to-all-start.1) | async-done | bytes 1048608 | tf_op jit(solution)/shard_map/all_to_all | solution.py:152
  294.0 1.1 convert_element_type.97
  295.2 2.1 copy.168
  297.5 6.7 %reduce-scatter.5.cloned.1.call-done = bf16[32,2,2048]{2,0,1:T(8,128)(2,1)} async-done(((bf16[32,2,4096]{2,0,1:T(8,128)(2,1)}), bf16[32,2,2048]{2,0,1:T(8,128)(2,1)}) %reduce-scatter.5.cloned.1.call-update) | async-done | bytes 262160 | tf_op jit(solution)/shard_map/reduce_scatter | solution.py:161
  304.2 1.0 convert_element_type.98
  (109 shorter events, 19.4 us)
Async XLA Ops:
  7.2 55.1 %copy-start = (bf16[4096,256]{1,0:T(8,128)(2,1)S(1)}, bf16[4096,256]{1,0:T(8,128)(2,1)}, u32[]{:S(2)}) copy-start(bf16[4096,256]{1,0:T(8,128)(2,1)} %param.26) | copy-start | bytes 6291460
  7.2 10.8 %copy-start.7 = (f32[32,3,256]{2,0,1:T(8,128)S(1)}, f32[32,3,256]{2,0,1:T(8,128)}, u32[]{:S(2)}) copy-start(f32[32,3,256]{2,0,1:T(8,128)} %param.23) | copy-start | bytes 294916
  7.2 10.9 %copy-start.13 = (f32[4,256]{1,0:T(4,128)S(1)}, f32[4,256]{1,0:T(4,128)}, u32[]{:S(2)}) copy-start(f32[4,256]{1,0:T(4,128)} %param.28) | copy-start | bytes 12292
  7.2 208.8 %reduce-scatter.3.cloned.1.call-start = ((), (), s32[]{:S(2)}) async-start(), calls=%async_computation.4 | async-start | bytes 4456448 | tf_op jit(solution)/shard_map/reduce_scatter | solution.py:120
  9.8 14.4 %collective-permute-start = (bf16[32,4096]{1,0:T(8,128)(2,1)S(1)}, bf16[32,4096]{1,0:T(8,128)(2,1)S(1)}, u32[]{:S(2)}, u32[]{:S(2)}) collective-permute-start(bf16[32,4096]{1,0:T(8,128)(2,1)S(1)} %all_gather.6), channel_id=1, source_target_pairs={{0,2},{2,4},{4,6},{6,8},{8,10},{10,12},{12,14},{14,0},{1,3},{3,5},... | collective-permute-start | bytes 786440 | tf_op jit(solution)/shard_map/ppermute | solution.py:20
  12.6 14.0 %collective-permute-start.1 = (bf16[32,4096]{1,0:T(8,128)(2,1)S(1)}, bf16[32,4096]{1,0:T(8,128)(2,1)S(1)}, u32[]{:S(2)}, u32[]{:S(2)}) collective-permute-start(bf16[32,4096]{1,0:T(8,128)(2,1)S(1)} %all_gather.6), channel_id=1, source_target_pairs={{0,14},{2,0},{4,2},{6,4},{8,6},{10,8},{12,10},{14,12},{1,15},{3,1}... | collective-permute-start | bytes 786440 | tf_op jit(solution)/shard_map/ppermute | solution.py:25
  24.2 13.2 %collective-permute-start.2 = (bf16[32,4096]{1,0:T(8,128)(2,1)S(1)}, bf16[32,4096]{1,0:T(8,128)(2,1)S(1)}, u32[]{:S(2)}, u32[]{:S(2)}) collective-permute-start(bf16[32,4096]{1,0:T(8,128)(2,1)S(1)} %collective-permute-done), channel_id=1, source_target_pairs={{0,2},{2,4},{4,6},{6,8},{8,10},{10,12},{12,14},{14,0},{1,3},{3,5},... | collective-permute-start | bytes 786440 | tf_op jit(solution)/shard_map/ppermute | solution.py:20
  26.6 13.2 %collective-permute-start.3 = (bf16[32,4096]{1,0:T(8,128)(2,1)S(1)}, bf16[32,4096]{1,0:T(8,128)(2,1)S(1)}, u32[]{:S(2)}, u32[]{:S(2)}) collective-permute-start(bf16[32,4096]{1,0:T(8,128)(2,1)S(1)} %collective-permute-done.1), channel_id=1, source_target_pairs={{0,14},{2,0},{4,2},{6,4},{8,6},{10,8},{12,10},{14,12},{1,15},{3,1}... | collective-permute-start | bytes 786440 | tf_op jit(solution)/shard_map/ppermute | solution.py:25
  37.3 12.4 %collective-permute-start.4 = (bf16[32,4096]{1,0:T(8,128)(2,1)S(1)}, bf16[32,4096]{1,0:T(8,128)(2,1)S(1)}, u32[]{:S(2)}, u32[]{:S(2)}) collective-permute-start(bf16[32,4096]{1,0:T(8,128)(2,1)S(1)} %collective-permute-done.2), channel_id=1, source_target_pairs={{0,2},{2,4},{4,6},{6,8},{8,10},{10,12},{12,14},{14,0},{1,3},{3,5},... | collective-permute-start | bytes 786440 | tf_op jit(solution)/shard_map/ppermute | solution.py:20
  39.8 13.2 %collective-permute-start.5 = (bf16[32,4096]{1,0:T(8,128)(2,1)S(1)}, bf16[32,4096]{1,0:T(8,128)(2,1)S(1)}, u32[]{:S(2)}, u32[]{:S(2)}) collective-permute-start(bf16[32,4096]{1,0:T(8,128)(2,1)S(1)} %collective-permute-done.3), channel_id=1, source_target_pairs={{0,14},{2,0},{4,2},{6,4},{8,6},{10,8},{12,10},{14,12},{1,15},{3,1}... | collective-permute-start | bytes 786440 | tf_op jit(solution)/shard_map/ppermute | solution.py:25
  43.6 18.7 %copy-start.19 = (f32[4096]{0:T(1024)S(1)}, f32[4096]{0:T(1024)}, u32[]{:S(2)}) copy-start(f32[4096]{0:T(1024)} %param.25) | copy-start | bytes 49156
  49.7 9.7 %collective-permute-start.6 = (bf16[32,4096]{1,0:T(8,128)(2,1)S(1)}, bf16[32,4096]{1,0:T(8,128)(2,1)S(1)}, u32[]{:S(2)}, u32[]{:S(2)}) collective-permute-start(bf16[32,4096]{1,0:T(8,128)(2,1)S(1)} %collective-permute-done.4), channel_id=1, source_target_pairs={{0,2},{2,4},{4,6},{6,8},{8,10},{10,12},{12,14},{14,0},{1,3},{3,5},... | collective-permute-start | bytes 786440 | tf_op jit(solution)/shard_map/ppermute | solution.py:20
  62.3 2.5 copy-start.16
  62.3 2.5 copy-start.14
  62.3 2.7 copy-start.4
  62.3 3.0 copy-start.11
  64.7 65.0 %copy-start.18 = (bf16[512,256]{1,0:T(8,128)(2,1)S(1)}, bf16[512,256]{1,0:T(8,128)(2,1)}, u32[]{:S(2)}) copy-start(bf16[512,256]{1,0:T(8,128)(2,1)} %param.32) | copy-start | bytes 786436
  64.7 64.9 %copy-start.21 = (f32[256]{0:T(256)S(1)}, f32[256]{0:T(256)}, u32[]{:S(2)}) copy-start(f32[256]{0:T(256)} %param.33) | copy-start | bytes 3076
  129.7 6.5 %copy-start.2 = (f32[32,16,256]{2,1,0:T(8,128)S(1)}, f32[32,16,256]{2,1,0:T(8,128)}, u32[]{:S(2)}) copy-start(f32[32,16,256]{2,1,0:T(8,128)} %param.24) | copy-start | bytes 1572868
  129.7 6.5 %copy-start.5 = (f32[16,256]{1,0:T(8,128)S(1)}, f32[16,256]{1,0:T(8,128)}, u32[]{:S(2)}) copy-start(f32[16,256]{1,0:T(8,128)} %param.34) | copy-start | bytes 49156
  134.4 2.5 copy-start.8
  134.4 2.5 copy-start.9
  136.2 3.4 %copy-start.15 = (f32[256]{0:T(256)S(1)}, f32[256]{0:T(256)}, u32[]{:S(2)}) copy-start(f32[256]{0:T(256)} %param.35) | copy-start | bytes 3076
  136.9 3.4 %copy-start.17 = (f32[256]{0:T(256)S(1)}, f32[256]{0:T(256)}, u32[]{:S(2)}) copy-start(f32[256]{0:T(256)} %copy-done.16) | copy-start | bytes 3076
  136.9 3.4 %copy-start.20 = (f32[4096]{0:T(1024)S(1)}, f32[4096]{0:T(1024)}, u32[]{:S(2)}) copy-start(f32[4096]{0:T(1024)} %param.25) | copy-start | bytes 49156
  140.4 3.2 %copy-start.1 = (bf16[256,4096]{1,0:T(8,128)(2,1)S(1)}, bf16[256,4096]{1,0:T(8,128)(2,1)}, u32[]{:S(2)}) copy-start(bf16[256,4096]{1,0:T(8,128)(2,1)} %param.36) | copy-start | bytes 6291460
  146.2 0.7 copy-start.12
  146.2 69.8 %copy-start.3 = (bf16[32,2048]{1,0:T(8,128)(2,1)S(1)}, bf16[32,2048]{1,0:T(8,128)(2,1)}, u32[]{:S(2)}) copy-start(bf16[32,2048]{1,0:T(8,128)(2,1)} %param.21) | copy-start | bytes 393220
  146.2 73.0 %copy-start.10 = (f32[4096]{0:T(1024)S(1)}, f32[4096]{0:T(1024)}, u32[]{:S(2)}) copy-start(f32[4096]{0:T(1024)} %param.37) | copy-start | bytes 49156
  263.7 29.2 %all-to-all-start.1 = ((bf16[1,8,16,4096]{3,2,0,1:T(8,128)(2,1)}), bf16[1,8,16,4096]{3,2,0,1:T(8,128)(2,1)S(1)}, u32[]{:S(2)}, u32[]{:S(2)}) async-start(bf16[1,8,16,4096]{3,2,0,1:T(8,128)(2,1)} %bitcast.141), calls=%async_computation.2 | async-start | bytes 2097152 | tf_op jit(solution)/shard_map/all_to_all | solution.py:152
  267.4 36.8 %reduce-scatter.5.cloned.1.call-start = ((), (), s32[]{:S(2)}) async-start(), calls=%async_computation.5 | async-start | bytes 786432 | tf_op jit(solution)/shard_map/reduce_scatter | solution.py:161
  294.0 3.3 %copy-start.6 = (bf16[4096,16]{0,1:T(8,128)(2,1)S(1)}, bf16[4096,16]{0,1:T(8,128)(2,1)}, u32[]{:S(2)}) copy-start(bf16[4096,16]{0,1:T(8,128)(2,1)} %param.38) | copy-start | bytes 393220
Sparse Core Ops, SparseCore 0:
  146.4 69.6 reduce-scatter.2
  297.4 6.7 reduce-scatter.4
